TPU v7x, 128 devices: a whole 4x4x4 slice. The times are simulated.
128 devices in a mesh: dp: 8 (over z, y_hi), head: 16 (over y_lo, x, core).
Axes of the slice: x: 4, y: 4 (y_hi: 2, y_lo: 2; y = y_hi * 2 + y_lo), z: 4, core: 2. Of those that a mesh axis runs over, the one named last changes fastest.
Arguments:
- ckpt_query: bfloat16 [4, 8192, 8192], P(None, ('dp', 'head')), may hold values from -0.125 to 0.125
- ckpt_key: bfloat16 [4, 8192, 1024], P(None, ('dp', 'head')), may hold values from -0.125 to 0.125
- ckpt_value: bfloat16 [4, 8192, 1024], P(None, ('dp', 'head')), may hold values from -0.125 to 0.125
- ckpt_output: bfloat16 [4, 8192, 8192], P(None, ('head', 'dp')), may hold values from -0.125 to 0.125
- hidden_in: bfloat16 [4096, 8192], P('dp'), may hold values from -17 to 17
- segment_ids: int32 [8, 512], P('dp'), may hold values from 0 to 3, never falling along the last dimension, each value on 1 to 256 neighbouring positions
Outputs:
- attn_out: bfloat16 [4096, 8192], P('dp', 'head')
All inputs are finite; a program needn't handle non-finite values.
Results may differ from a plain program's by a relative error of at most 0.01.
The roundings to bfloat16 on the way count: a program that leaves them out, or rounds other values in their place, can miss the bound.
Values may be sent and summed in bfloat16 or wider, within the bound.
A program may use at most 128 MiB of HBM per device.

v0:
```python
import jax
import jax.numpy as jnp
from jax import lax
from jax.sharding import PartitionSpec as P

rope_base = 500000.0


def average(stack):
    return (jnp.sum(stack.astype(jnp.float32), axis=0) * 0.25).astype(jnp.bfloat16)


def rotate(values, positions):
    half = values.shape[-1] // 2
    freq = rope_base ** (-2.0 * jnp.arange(half, dtype=jnp.float32) / values.shape[-1])
    angle = positions[:, None] * freq[None, :]
    cosine = jnp.cos(angle)[:, None, :]
    sine = jnp.sin(angle)[:, None, :]
    first = values[..., :half]
    second = values[..., half:]
    return jnp.concatenate(
        [first * cosine - second * sine, second * cosine + first * sine], axis=-1
    )


def shards(ckpt_query, ckpt_key, ckpt_value, ckpt_output, hidden_in, segment_ids):
    n_dp = lax.axis_size("dp")
    n_head = lax.axis_size("head")
    rows, wide = ckpt_query.shape[1:]
    kv_wide = ckpt_key.shape[2]
    output_rows = lax.all_gather(average(ckpt_output), "dp", axis=0, tiled=True)
    mean_query = average(ckpt_query).reshape(rows, n_head, wide // n_head)
    mean_key = average(ckpt_key).reshape(rows, n_head, kv_wide // n_head)
    mean_value = average(ckpt_value).reshape(rows, n_head, kv_wide // n_head)
    packed = jnp.concatenate([mean_query, mean_key, mean_value], axis=2).transpose(1, 0, 2)
    moved = lax.all_to_all(packed, "head", split_axis=0, concat_axis=0, tiled=True)
    gathered = lax.all_gather(moved.reshape(n_head * rows, -1), "dp", axis=0, tiled=True)
    tok = hidden_in.shape[0]
    projected = jnp.dot(hidden_in, gathered, preferred_element_type=jnp.float32)
    query = projected[:, : wide // n_head]
    head_size = 2 * kv_wide // n_head
    own = projected[:, wide // n_head :]
    position = lax.axis_index("head")
    other = lax.ppermute(own, "head", [(i, i ^ 1) for i in range(n_head)])
    half = head_size // 2
    lower = position % 2 == 0
    low = jnp.where(lower, own, other)
    high = jnp.where(lower, other, own)
    keys = jnp.concatenate([low[:, :half], high[:, :half]], axis=1)
    values = jnp.concatenate([low[:, half:], high[:, half:]], axis=1)
    heads_here = query.shape[1] // head_size
    positions = jnp.arange(tok, dtype=jnp.float32)
    q_rot = rotate(query.reshape(tok, heads_here, head_size), positions).astype(jnp.bfloat16)
    k_rot = rotate(keys.reshape(tok, 1, head_size), positions)[:, 0].astype(jnp.bfloat16)
    v_b = values.astype(jnp.bfloat16)
    scores = jnp.einsum(
        "qhd,kd->hqk", q_rot, k_rot, preferred_element_type=jnp.float32
    ) * head_size ** (-0.5)
    order = jnp.arange(tok, dtype=jnp.int32)
    segment = segment_ids[0]
    allowed = (order[:, None] >= order[None, :]) & (segment[:, None] == segment[None, :])
    scores = jnp.where(allowed[None], scores, -1e30)
    peak = jnp.max(scores, axis=-1, keepdims=True)
    weights = jnp.exp(scores - peak)
    probs = (weights / jnp.sum(weights, axis=-1, keepdims=True)).astype(jnp.bfloat16)
    context = jnp.einsum("hqk,kd->qhd", probs, v_b, preferred_element_type=jnp.float32)
    context = context.astype(jnp.bfloat16).reshape(tok, heads_here * head_size)
    everyone = lax.all_gather(context, "head", axis=0)
    weight = output_rows.reshape(output_rows.shape[0], n_head, wide // n_head)
    result = lax.dot_general(
        everyone, weight, (((0, 2), (1, 2)), ((), ())), preferred_element_type=jnp.float32
    )
    return result.astype(jnp.bfloat16)


def solution(mesh):
    placed = (
        P(None, ("dp", "head"), None),
        P(None, ("dp", "head"), None),
        P(None, ("dp", "head"), None),
        P(None, ("head", "dp"), None),
        P("dp", None),
        P("dp", None),
    )
    return jax.shard_map(
        shards, mesh=mesh, in_specs=placed, out_specs=P("dp", "head"), check_vma=False
    )
```

profile of v0, /device:TPU:1, one launch (start us, length us, event | category | flops | bytes accessed | tf_op | source)
XLA Modules:
  0.0 342.0 jit_solution(17139786216191566086)
XLA Ops:
  6.5 0.0 all-gather.4.cloned.1.call-start
  6.5 1.1 convert_reduce_fusion.3
  7.7 0.2 convert_element_type.59
  7.9 1.2 convert_reduce_fusion.2
  9.1 0.2 convert_element_type.62
  9.3 3.2 convert_reduce_fusion.1
  12.4 0.1 multiply_convert_fusion.1
  12.6 0.4 copy.40
  12.9 0.2 maximum_bitcast_fusion
  13.1 0.3 copy.26
  13.4 25.1 %all_to_all.5 = bf16[16,64,640]{2,1,0:T(8,128)(2,1)} all-to-all(bf16[16,64,640]{2,1,0:T(8,128)(2,1)S(1)} %copy.26), channel_id=1, replica_groups=mesh['dp'=8,'head'=16] {'head'}, dimensions={0} | all-to-all | bytes 2621440 | tf_op jit(solution)/shard_map/all_to_all | solution.py:36
  38.6 0.0 all-gather.4.cloned.1.call-update
  38.6 0.0 copy-start.1
  38.6 0.0 all-gather.8.cloned.1.call-start
  38.6 3.2 convert_reduce_fusion
  41.8 1.2 multiply_convert_fusion
  43.0 0.0 all-gather.8.cloned.1.call-update
  43.0 0.0 all-gather.6.cloned.1.call-start
  43.1 0.0 copy-done.1
  43.1 0.2 fusion.8
  43.3 1.0 fusion.14
  44.3 120.4 %all-gather.4.cloned.1.call-done = bf16[8192,640]{1,0:T(8,128)(2,1)} async-done(((bf16[1024,640]{1,0:T(8,128)(2,1)}), bf16[8192,640]{1,0:T(8,128)(2,1)}) %all-gather.4.cloned.1.call-update) | async-done | bytes 10485776 | tf_op jit(solution)/shard_map/all_gather | solution.py:37
  164.6 11.2 %convolution_bitcast_fusion = f32[512,640]{0,1:T(8,128)S(1)} fusion(bf16[8192,640]{1,0:T(8,128)(2,1)} %all-gather.4.cloned.1.call-done, bf16[512,8192]{1,0:T(8,128)(2,1)} %param.10), kind=kOutput, calls=%fused_computation.13 | convolution fusion | flops 5368709120 | bytes 20185088 | tf_op jit(solution)/shard_map/dot_general | solution.py:39
  175.9 0.0 copy-start
  175.9 0.8 slice.42
  176.7 0.1 slice.49
  176.8 1.3 collective-permute-start
  178.1 0.1 fusion.25
  178.2 0.0 copy-done
  178.2 0.3 copy.39
  178.6 0.3 copy.38
  178.9 0.3 subtract_convert_fusion
  179.2 0.4 collective-permute-done
  179.6 1.1 broadcast_select_fusion.1
  180.8 0.6 subtract_convert_fusion.1
  181.4 0.8 fusion.9
  182.1 2.1 fusion.26
  184.3 0.5 fusion.6
  184.8 1.0 copy.31
  185.8 0.0 all-gather.6.cloned.1.call-update
  185.8 86.2 %all-gather.8.cloned.1.call-done = bf16[512,8192]{1,0:T(8,128)(2,1)} async-done(((bf16[64,8192]{1,0:T(8,128)(2,1)}), bf16[512,8192]{1,0:T(8,128)(2,1)}) %all-gather.8.cloned.1.call-update) | async-done | bytes 8388624 | tf_op jit(solution)/shard_map/all_gather | solution.py:31
  272.0 12.0 %copy.32 = bf16[512,8192]{0,1:T(8,128)(2,1)} copy(bf16[512,8192]{1,0:T(8,128)(2,1)} %all-gather.8.cloned.1.call-done) | data formatting | bytes 16777216 | tf_op jit(solution)/shard_map/all_gather | solution.py:31
  284.1 40.3 %all-gather.6.cloned.1.call-done = bf16[16,512,512]{2,1,0:T(8,128)(2,1)} async-done(((bf16[1,512,512]{2,1,0:T(8,128)(2,1)}), bf16[16,512,512]{2,1,0:T(8,128)(2,1)}) %all-gather.6.cloned.1.call-update) | async-done | bytes 8388624 | tf_op jit(solution)/shard_map/all_gather | solution.py:68
  324.4 11.0 %fusion.7 = bf16[512,512]{1,0:T(8,128)(2,1)} fusion(bf16[16,512,512]{2,1,0:T(8,128)(2,1)} %all-gather.6.cloned.1.call-done, bf16[512,16,512]{0,2,1:T(8,128)(2,1)} %bitcast.42), kind=kOutput, calls=%fused_computation.17 | convolution fusion | flops 4295229440 | bytes 17301504 | tf_op jit(solution)/shard_map/dot_general | solution.py:70
  (8 shorter events, 0.1 us)
Async XLA Ops:
  6.5 158.1 %all-gather.4.cloned.1.call-start = ((), (), s32[]{:S(2)}) async-start(), calls=%async_computation.1 | async-start | bytes 11796480 | tf_op jit(solution)/shard_map/all_gather | solution.py:37
  38.6 4.5 %copy-start.1 = (s32[1,512]{1,0:T(1,128)S(1)}, s32[1,512]{1,0:T(1,128)}, u32[]{:S(2)}) copy-start(s32[1,512]{1,0:T(1,128)} %param.11) | copy-start | bytes 6148
  38.6 233.4 %all-gather.8.cloned.1.call-start = ((), (), s32[]{:S(2)}) async-start(), calls=%async_computation.3 | async-start | bytes 9437184 | tf_op jit(solution)/shard_map/all_gather | solution.py:31
  43.0 281.4 %all-gather.6.cloned.1.call-start = ((), (), s32[]{:S(2)}) async-start(), calls=%async_computation.2 | async-start | bytes 8912896 | tf_op jit(solution)/shard_map/all_gather | solution.py:68
  175.9 2.3 copy-start
  176.8 2.8 collective-permute-start
Sparse Core Ops, SparseCore 0:
  38.7 125.9 all-gather.3
  167.0 104.9 all-gather.7
  273.7 50.6 all-gather.5
where the time goes:
time: 343 us; the launch traced here: 342 us
  waiting for transfers between devices  247 us (72%)
  blocking collectives  25.1 us (7%)
  matrix products  23.5 us (7%)
  local copies, waits for them, and re-layouts  15.7 us (5%)
  other arithmetic  15.4 us (4%)
  between operations  13.3 us (4%)
    all_gather x1, waiting for transfers between devices, shards(): lax.all_gather(moved.reshape(n_head * rows, -1), 'dp', axis=0, tiled=True)  120 us
    all_gather x1, waiting for transfers between devices, shards(): output_rows = lax.all_gather(average(ckpt_output), 'dp', axis=0, tiled=True)  86.2 us
    all_gather x1, waiting for transfers between devices, shards(): everyone = lax.all_gather(context, 'head', axis=0)  40.3 us
    all_to_all x1, blocking collectives, shards(): lax.all_to_all(packed, 'head', split_axis=0, concat_axis=0, tiled=True)  25.1 us
    all_gather x1, local copies, waits for them, and re-layouts, shards(): output_rows = lax.all_gather(average(ckpt_output), 'dp', axis=0, tiled=True)  12 us
    dot_general x1, matrix products, shards(): projected = jnp.dot(hidden_in, gathered, preferred_element_type=jnp.float32)  11.2 us
    dot_general x1, matrix products, shards(): lax.dot_general(everyone, weight, (((0, 2), (1, 2)), ((), ())), preferred...  11 us
    reduce_sum x4, other arithmetic, average(): jnp.sum(stack.astype(jnp.float32), axis=0) * 0.25  8.62 us
  transfers between devices with their start and end apart: 4, of which 4 were waited for; matrix products, arithmetic and copies ran while one was open for 11% of the time, Pallas kernels for 0%

commit v1 on v0

--- a/solution.py
+++ b/solution.py
@@ -28,7 +28,9 @@
     n_head = lax.axis_size("head")
     rows, wide = ckpt_query.shape[1:]
     kv_wide = ckpt_key.shape[2]
-    output_rows = lax.all_gather(average(ckpt_output), "dp", axis=0, tiled=True)
+    output_rows = jnp.concatenate(
+        lax.all_to_all(jnp.stack([average(ckpt_output)] * lax.axis_size("dp")), "dp", 0, 0), axis=0
+    )
     mean_query = average(ckpt_query).reshape(rows, n_head, wide // n_head)
     mean_key = average(ckpt_key).reshape(rows, n_head, kv_wide // n_head)
     mean_value = average(ckpt_value).reshape(rows, n_head, kv_wide // n_head)

time: 343 us -> 362 us (1.055)
  blocking collectives: 25.1 us -> 163 us
  waiting for transfers between devices: 247 us -> 125 us
  matrix products: 23.5 us -> 28.8 us
    all_to_all x0 -> x1, blocking collectives: none -> 137 us  [shards(): lax.all_to_all(jnp.stack([average(ckpt_output)] * lax.axis_size('dp')), '...]
    all_gather x1 -> x0, waiting for transfers between devices: 86.2 us -> none  [shards(): output_rows = lax.all_gather(average(ckpt_output), 'dp', axis=0, tiled=True)]
    all_gather x1, waiting for transfers between devices: 40.3 us -> 0.01 us  [shards(): everyone = lax.all_gather(context, 'head', axis=0)]
    all_gather x1 -> x0, local copies, waits for them, and re-layouts: 12 us -> none  [shards(): output_rows = lax.all_gather(average(ckpt_output), 'dp', axis=0, tiled=True)]
    unnamed x7 -> x8, local copies, waits for them, and re-layouts: 1.03 us -> 12 us
    dot_general x1, matrix products: 11 us -> 16.3 us  [shards(): lax.dot_general(everyone, weight, (((0, 2), (1, 2)), ((), ())), preferred...]
    all_gather x1, waiting for transfers between devices: 120 us -> 125 us  [shards(): lax.all_gather(moved.reshape(n_head * rows, -1), 'dp', axis=0, tiled=True)]
  transfers between devices with their start and end apart: 4 -> 3, of which waited for: 4 -> 2; matrix products, arithmetic and copies ran while one was open for 11% -> 5% of each run, Pallas kernels for 0% -> 0%
where the time goes in v1:
time: 362 us
  blocking collectives  163 us (45%)
  waiting for transfers between devices  125 us (35%)
  matrix products  28.8 us (8%)
  local copies, waits for them, and re-layouts  15.7 us (4%)
  other arithmetic  14.4 us (4%)
  between operations  13.7 us (4%)
    all_to_all x1, blocking collectives, shards(): lax.all_to_all(jnp.stack([average(ckpt_output)] * lax.axis_size('dp')), '...  137 us
    all_gather x1, waiting for transfers between devices, shards(): lax.all_gather(moved.reshape(n_head * rows, -1), 'dp', axis=0, tiled=True)  125 us
    all_to_all x1, blocking collectives, shards(): lax.all_to_all(packed, 'head', split_axis=0, concat_axis=0, tiled=True)  25.1 us
    dot_general x1, matrix products, shards(): lax.dot_general(everyone, weight, (((0, 2), (1, 2)), ((), ())), preferred...  16.3 us
    unnamed x8, local copies, waits for them, and re-layouts  12 us
    dot_general x1, matrix products, shards(): projected = jnp.dot(hidden_in, gathered, preferred_element_type=jnp.float32)  11.2 us
    reduce_sum x4, other arithmetic, average(): jnp.sum(stack.astype(jnp.float32), axis=0) * 0.25  8.62 us
  transfers between devices with their start and end apart: 3, of which 2 were waited for; matrix products, arithmetic and copies ran while one was open for 5% of the time, Pallas kernels for 0%

profile of v1, /device:TPU:1, one launch (start us, length us, event | category | flops | bytes accessed | tf_op | source)
XLA Modules:
  0.0 361.7 jit_solution(1842490860181930722)
XLA Ops:
  6.5 0.0 all-gather.3.cloned.1.call-start
  6.5 1.1 convert_reduce_fusion.3
  7.7 0.2 convert_element_type.61
  7.9 1.2 convert_reduce_fusion.2
  9.1 0.2 convert_element_type.64
  9.3 3.2 convert_reduce_fusion.1
  12.4 0.1 multiply_convert_fusion.1
  12.6 0.4 copy.37
  12.9 0.0 copy-start.1
  12.9 0.2 maximum_bitcast_fusion
  13.1 0.3 copy.25
  13.4 25.1 %all_to_all.10 = bf16[16,64,640]{2,1,0:T(8,128)(2,1)} all-to-all(bf16[16,64,640]{2,1,0:T(8,128)(2,1)S(1)} %copy.25), channel_id=1, replica_groups=mesh['dp'=8,'head'=16] {'head'}, dimensions={0} | all-to-all | bytes 2621440 | tf_op jit(solution)/shard_map/all_to_all | solution.py:38
  38.6 0.0 all-gather.3.cloned.1.call-update
  38.6 0.0 all-gather.5.cloned.1.call-start
  38.7 0.0 copy-done.1
  38.7 0.2 fusion.15
  38.9 1.0 fusion.21
  39.9 124.8 %all-gather.3.cloned.1.call-done = bf16[8192,640]{1,0:T(8,128)(2,1)} async-done(((bf16[1024,640]{1,0:T(8,128)(2,1)}), bf16[8192,640]{1,0:T(8,128)(2,1)}) %all-gather.3.cloned.1.call-update) | async-done | bytes 10485776 | tf_op jit(solution)/shard_map/all_gather | solution.py:39
  164.7 11.2 %convolution_bitcast_fusion = f32[512,640]{0,1:T(8,128)S(1)} fusion(bf16[8192,640]{1,0:T(8,128)(2,1)} %all-gather.3.cloned.1.call-done, bf16[512,8192]{1,0:T(8,128)(2,1)} %param.10), kind=kOutput, calls=%fused_computation.15 | convolution fusion | flops 5368709120 | bytes 20185088 | tf_op jit(solution)/shard_map/dot_general | solution.py:41
  175.9 0.0 copy-start
  175.9 0.8 slice.42
  176.7 0.1 slice.49
  176.7 1.3 collective-permute-start
  178.1 0.1 fusion.32
  178.2 0.0 copy-done
  178.2 0.3 copy.36
  178.5 0.3 copy.35
  178.9 0.3 subtract_convert_fusion
  179.2 0.4 collective-permute-done
  179.6 1.1 broadcast_select_fusion.1
  180.8 0.6 subtract_convert_fusion.1
  181.3 0.8 fusion.16
  182.1 2.1 fusion.33
  184.3 0.5 fusion.14
  184.8 1.0 copy.30
  185.8 0.0 all-gather.5.cloned.1.call-update
  185.8 3.2 convert_reduce_fusion
  188.9 0.1 multiply_convert_fusion
  189.1 1.1 stack.2
  190.2 137.4 %all_to_all.11 = bf16[8,64,8192]{2,1,0:T(8,128)(2,1)} all-to-all(bf16[8,64,8192]{2,1,0:T(8,128)(2,1)S(1)} %stack.2), channel_id=1, replica_groups=mesh['dp'=8,'head'=16] {'dp'}, dimensions={0} | all-to-all | bytes 16777216 | tf_op jit(solution)/shard_map/all_to_all | solution.py:32
  327.6 11.0 %copy.38 = bf16[64,8,16,512]{3,2,1,0:T(8,128)(2,1)} copy(bf16[64,8,16,512]{3,1,2,0:T(8,128)(2,1)} %bitcast.43) | data formatting | bytes 16777216
  338.6 0.0 all-gather.5.cloned.1.call-done
  338.6 16.3 %fusion.11 = bf16[512,512]{1,0:T(8,128)(2,1)} fusion(bf16[16,512,512]{2,1,0:T(8,128)(2,1)} %all-gather.5.cloned.1.call-done, bf16[512,16,512]{2,1,0:T(8,128)(2,1)} %bitcast.44), kind=kOutput, calls=%fused_computation.18 | convolution fusion | flops 4295229440 | bytes 17301504 | tf_op jit(solution)/shard_map/dot_general | solution.py:72
  (8 shorter events, 0.1 us)
Async XLA Ops:
  6.5 158.1 %all-gather.3.cloned.1.call-start = ((), (), s32[]{:S(2)}) async-start(), calls=%async_computation.2 | async-start | bytes 11796480 | tf_op jit(solution)/shard_map/all_gather | solution.py:39
  12.9 25.8 %copy-start.1 = (s32[1,512]{1,0:T(1,128)S(1)}, s32[1,512]{1,0:T(1,128)}, u32[]{:S(2)}) copy-start(s32[1,512]{1,0:T(1,128)} %param.11) | copy-start | bytes 6148
  38.6 300.0 %all-gather.5.cloned.1.call-start = ((), (), s32[]{:S(2)}) async-start(), calls=%async_computation.3 | async-start | bytes 8912896 | tf_op jit(solution)/shard_map/all_gather | solution.py:70
  175.9 2.3 copy-start
  176.7 2.8 collective-permute-start
Sparse Core Ops, SparseCore 0:
  38.7 125.9 all-gather.2
  185.9 89.0 all-gather.4
